TPU v7x, 32 devices: a whole 2x2x4 slice. The times are simulated.
32 devices in a mesh: groups: 2 (over x), probe: 16 (over z, y, core).
Axes of the slice: x: 2, y: 2, z: 4, core: 2. Of those that a mesh axis runs over, the one named last changes fastest.
Arguments:
- atom_positions: float32 [2, 32768], P(None, ('groups', 'probe')), parts along dimension 1, may hold values from 0 to 512
- atom_species: int32 [32768], P(('groups', 'probe')), parts along dimension 0, may hold values from 0 to 7
- atom_slice: int32 [32768], P(('groups', 'probe')), parts along dimension 0, may hold values from 0 to 3
- species_amp: float32 [8], replicated, may hold values from 0.02 to 0.125
- species_width: float32 [8], replicated, may hold values from 2 to 8
- probe_spectrum: float32 [2, 256, 256], replicated, may hold values from -6 to 6
- window_offsets: int32 [128, 2], P(('groups', 'probe')), parts along dimension 0, may hold values from 0 to 256
- probe_shifts: int32 [128, 2], P(('groups', 'probe')), parts along dimension 0, may hold values from 0 to 255
- slice_phase: float32 [3], replicated, may hold values from 0.0002746582 to 0.001373291
Outputs:
- scan_spectrum: float32 [2, 128, 65536], P(None, 'groups', 'probe'), parts along dimension 1
There are 2 independent parts, one for each index of `groups`. A program takes and returns all parts, laid end to end along the dimension named above; an argument that names none is the same for every part. Nothing has to cross between parts.
All inputs are finite; a program needn't handle non-finite values.
Results may differ from a plain program's by a relative error of at most 0.025.
Values may be sent and summed in bfloat16 or wider, within the bound.
No kernel may reach another device: no remote copies, remote signals or barrier semaphores. Data moves between devices by JAX's collectives and lax.ppermute only.
A program may use at most 64 MiB of HBM per device.

v0:
```python
import math
import jax
import jax.numpy as jnp
from jax import lax
from jax.sharding import PartitionSpec as P

G = 512
W = 256
SLICES = 4


def dft_tables(length):
    indices = jnp.arange(length, dtype=jnp.int32)
    angles = (
        2.0 * math.pi / length * (indices[:, None] * indices[None, :] % length).astype(jnp.float32)
    )
    factor = 1.0 / math.sqrt(length)
    return (
        (jnp.cos(angles) * factor).astype(jnp.bfloat16),
        (jnp.sin(angles) * factor).astype(jnp.bfloat16),
    )


def along_rows(real_part, imag_part, matrix, direction):
    batch_count = real_part.shape[0]
    length = real_part.shape[1]
    stacked = jnp.concatenate([real_part, imag_part], axis=0)
    product = jnp.einsum("ky,byx->bkx", matrix, stacked, preferred_element_type=jnp.float32)
    new_real = product[:batch_count, :length] - direction * product[batch_count:, length:]
    new_imag = product[batch_count:, :length] + direction * product[:batch_count, length:]
    return (new_real, new_imag)


def along_columns(real_part, imag_part, matrix, direction):
    batch_count = real_part.shape[0]
    length = real_part.shape[2]
    stacked = jnp.concatenate([real_part, imag_part], axis=0)
    product = jnp.einsum("byx,xl->byl", stacked, matrix, preferred_element_type=jnp.float32)
    new_real = product[:batch_count, :, :length] - direction * product[batch_count:, :, length:]
    new_imag = product[batch_count:, :, :length] + direction * product[:batch_count, :, length:]
    return (new_real, new_imag)


def transmit(real_part, imag_part, window):
    values = window.astype(jnp.float32)
    cosine = jnp.cos(values)
    sine = jnp.sin(values)
    return (
        (real_part * cosine - imag_part * sine).astype(jnp.bfloat16),
        (real_part * sine + imag_part * cosine).astype(jnp.bfloat16),
    )


def frequencies(length):
    indices = jnp.arange(length, dtype=jnp.int32)
    frequency = (indices + length // 2) % length - length // 2
    squared = frequency[:, None] * frequency[:, None] + frequency[None, :] * frequency[None, :]
    aperture = (9 * squared < length * length).astype(jnp.float32)
    return (squared.astype(jnp.float32), aperture)


def multislice(probe_spectrum, shifts, windows, slice_phase):
    length = probe_spectrum.shape[-1]
    cos_table, sin_table = dft_tables(length)
    rows_matrix = jnp.concatenate([cos_table, sin_table], axis=0)
    columns_matrix = jnp.concatenate([cos_table, sin_table], axis=1)
    squared, aperture = frequencies(length)
    indices = jnp.arange(length, dtype=jnp.int32)
    phase_index = (
        indices[None, :, None] * shifts[:, 0][:, None, None]
        + indices[None, None, :] * shifts[:, 1][:, None, None]
    ) % length
    angles = 2.0 * math.pi / length * phase_index.astype(jnp.float32)
    cosine = jnp.cos(angles)
    sine = jnp.sin(angles)
    real_part = (probe_spectrum[0] * cosine + probe_spectrum[1] * sine).astype(jnp.bfloat16)
    imag_part = (probe_spectrum[1] * cosine - probe_spectrum[0] * sine).astype(jnp.bfloat16)
    real_part, imag_part = along_rows(real_part, imag_part, rows_matrix, 1.0)
    real_part, imag_part = along_columns(
        real_part.astype(jnp.bfloat16), imag_part.astype(jnp.bfloat16), columns_matrix, 1.0
    )
    real_part, imag_part = transmit(real_part, imag_part, windows[0])
    for layer in range(len(windows) - 1):
        real_part, imag_part = along_rows(real_part, imag_part, rows_matrix, -1.0)
        real_part, imag_part = along_columns(
            real_part.astype(jnp.bfloat16), imag_part.astype(jnp.bfloat16), columns_matrix, -1.0
        )
        phases = slice_phase[layer] * squared
        prop_real = aperture * jnp.cos(phases)
        prop_imag = -aperture * jnp.sin(phases)
        new_real = (real_part * prop_real - imag_part * prop_imag).astype(jnp.bfloat16)
        new_imag = (real_part * prop_imag + imag_part * prop_real).astype(jnp.bfloat16)
        real_part, imag_part = along_rows(new_real, new_imag, rows_matrix, 1.0)
        real_part, imag_part = along_columns(
            real_part.astype(jnp.bfloat16), imag_part.astype(jnp.bfloat16), columns_matrix, 1.0
        )
        real_part, imag_part = transmit(real_part, imag_part, windows[layer + 1])
    real_part, imag_part = along_rows(real_part, imag_part, rows_matrix, -1.0)
    real_part, imag_part = along_columns(
        real_part.astype(jnp.bfloat16), imag_part.astype(jnp.bfloat16), columns_matrix, -1.0
    )
    return (aperture * (real_part * real_part + imag_part * imag_part)).astype(jnp.bfloat16)


def atom_factors(
    atom_positions, atom_species, atom_slice, species_amp, species_width, grid, layers
):
    species_ids = jnp.arange(species_amp.shape[0], dtype=jnp.int32)
    selector = (atom_species[:, None] == species_ids[None, :]).astype(jnp.float32)
    amplitude = jnp.sum(selector * species_amp[None, :], axis=1)
    widths = jnp.sum(selector * species_width[None, :], axis=1)
    inverse_spread = 0.5 / (widths * widths)
    pixels = jnp.arange(grid, dtype=jnp.float32)
    along_y = jnp.exp(
        -jnp.square(pixels[:, None] - atom_positions[0][None, :]) * inverse_spread[None, :]
    )
    layer_ids = jnp.arange(layers, dtype=jnp.int32)
    weight = amplitude[None, :] * (atom_slice[None, :] == layer_ids[:, None]).astype(jnp.float32)
    row_factor = (
        (weight[:, None, :] * along_y[None, :, :]).astype(jnp.bfloat16).reshape(layers * grid, -1)
    )
    column_factor = jnp.exp(
        -jnp.square(pixels[None, :] - atom_positions[1][:, None]) * inverse_spread[:, None]
    ).astype(jnp.bfloat16)
    return (row_factor, column_factor)


def scan_transform(received):
    intensity = received[:, 0, :]
    positions = intensity.shape[0]
    cos_scan, sin_scan = dft_tables(positions)
    matrix = jnp.concatenate([cos_scan, sin_scan], axis=0)
    product = jnp.dot(matrix, intensity, preferred_element_type=jnp.float32)
    return jnp.stack([product[:positions], -product[positions:]], axis=0)


def on_device(
    atom_positions,
    atom_species,
    atom_slice,
    species_amp,
    species_width,
    probe_spectrum,
    window_offsets,
    probe_shifts,
    slice_phase,
):
    devices = lax.axis_size("probe")
    row_factor, column_factor = atom_factors(
        atom_positions, atom_species, atom_slice, species_amp, species_width, G, SLICES
    )
    partial_field = jnp.dot(row_factor, column_factor, preferred_element_type=jnp.float32)
    whole_field = lax.psum(partial_field, "probe").astype(jnp.bfloat16).reshape(SLICES, G, G)
    slabs = [whole_field[layer] for layer in range(SLICES)]
    windows = []
    for slab in slabs:
        windows.append(
            jax.vmap(lambda corner: lax.dynamic_slice(slab, (corner[0], corner[1]), (W, W)))(
                window_offsets
            )
        )
    intensity = multislice(probe_spectrum, probe_shifts, windows, slice_phase)
    local_count = intensity.shape[0]
    pieces = intensity.reshape(local_count, devices, W * W // devices)
    return scan_transform(lax.all_to_all(pieces, "probe", split_axis=1, concat_axis=0, tiled=True))


def solution(mesh):
    placed = (
        P(None, ("groups", "probe")),
        P(("groups", "probe")),
        P(("groups", "probe")),
        P(),
        P(),
        P(),
        P(("groups", "probe"), None),
        P(("groups", "probe"), None),
        P(),
    )
    return jax.shard_map(
        on_device, mesh=mesh, in_specs=placed, out_specs=P(None, "groups", "probe"), check_vma=False
    )
```

profile of v0, /device:TPU:0, one launch (start us, length us, event | category | flops | bytes accessed | tf_op | source)
XLA Modules:
  0.0 217.3 jit_solution(16012172392962101634)
XLA Ops:
  5.0 4.6 %fusion.16 = f32[2048,512]{1,0:T(8,128)} fusion(bf16[2048,1024]{1,0:T(8,128)(2,1)S(1)} %bitcast.101, f32[1024]{0:T(1024)S(1)} %multiply_divide_fusion, f32[1024]{0:T(1024)S(1)} %bitcast.104), kind=kOutput, calls=%fused_computation.49 | convolution fusion | flops 2150105088 | bytes 8396800 | tf_op jit(solution)/shard_map/dot_general | solution.py:152
  9.5 97.1 %all-reduce.1 = bf16[2048,512]{1,0:T(8,128)(2,1)S(1)} all-reduce(f32[2048,512]{1,0:T(8,128)} %fusion.16), channel_id=1, replica_groups=mesh['groups'=2,'probe'=16] {'probe'}, use_global_device_ids=true, to_apply=%region_2.0 | all-reduce | flops 1048576 | bytes 6291456 | tf_op jit(solution)/shard_map/psum | solution.py:153
  107.8 11.6 %while.7 = (s32[]{:T(128)}, bf16[512,512]{1,0:T(8,128)(2,1)}, s32[4,2]{0,1:T(2,128)S(1)}, bf16[4,256,256]{2,1,0:T(8,128)(2,1)S(1)}, s32[]{:T(128)}) while((s32[]{:T(128)}, bf16[512,512]{1,0:T(8,128)(2,1)}, s32[4,2]{0,1:T(2,128)S(1)}, bf16[4,256,256]{2,1,0:T(8,128)(2,1)S(1)}, s32[]{:T(128)}) %tuple.96), condition=%wide.while_cond.3, body=%wide.while_body.3.sunk | while | flops 2 | bytes 262261 | solution.py:158
  108.5 2.2 %bitcast_dynamic-update-slice_fusion.11 = bf16[4,256,256]{2,1,0:T(8,128)(2,1)S(1)} fusion(bf16[4,256,256]{2,1,0:T(8,128)(2,1)S(1)} %get-tuple-element.264, s32[]{:T(128)S(6)} %copy.159, bf16[512,512]{1,0:T(8,128)(2,1)} %get-tuple-element.267, s32[]{:T(128)} %bitcast.99, s32[]{:T(128)} %bitcast.100), kind=kLoop, calls=%fused_computation.6.clone.1 | loop fusion | bytes 262156 | tf_op jit(solution)/shard_map/vmap()/gather
  111.4 2.2 %bitcast_dynamic-update-slice_fusion.11 = bf16[4,256,256]{2,1,0:T(8,128)(2,1)S(1)} fusion(bf16[4,256,256]{2,1,0:T(8,128)(2,1)S(1)} %get-tuple-element.264, s32[]{:T(128)S(6)} %copy.159, bf16[512,512]{1,0:T(8,128)(2,1)} %get-tuple-element.267, s32[]{:T(128)} %bitcast.99, s32[]{:T(128)} %bitcast.100), kind=kLoop, calls=%fused_computation.6.clone.1 | loop fusion | bytes 262156 | tf_op jit(solution)/shard_map/vmap()/gather
  114.3 2.2 %bitcast_dynamic-update-slice_fusion.11 = bf16[4,256,256]{2,1,0:T(8,128)(2,1)S(1)} fusion(bf16[4,256,256]{2,1,0:T(8,128)(2,1)S(1)} %get-tuple-element.264, s32[]{:T(128)S(6)} %copy.159, bf16[512,512]{1,0:T(8,128)(2,1)} %get-tuple-element.267, s32[]{:T(128)} %bitcast.99, s32[]{:T(128)} %bitcast.100), kind=kLoop, calls=%fused_computation.6.clone.1 | loop fusion | bytes 262156 | tf_op jit(solution)/shard_map/vmap()/gather
  117.1 2.2 %bitcast_dynamic-update-slice_fusion.11 = bf16[4,256,256]{2,1,0:T(8,128)(2,1)S(1)} fusion(bf16[4,256,256]{2,1,0:T(8,128)(2,1)S(1)} %get-tuple-element.264, s32[]{:T(128)S(6)} %copy.159, bf16[512,512]{1,0:T(8,128)(2,1)} %get-tuple-element.267, s32[]{:T(128)} %bitcast.99, s32[]{:T(128)} %bitcast.100), kind=kLoop, calls=%fused_computation.6.clone.1 | loop fusion | bytes 262156 | tf_op jit(solution)/shard_map/vmap()/gather
  120.1 11.9 %while.6 = (s32[]{:T(128)}, bf16[512,512]{1,0:T(8,128)(2,1)}, s32[4,2]{0,1:T(2,128)S(1)}, bf16[4,256,256]{2,1,0:T(8,128)(2,1)S(1)}, s32[]{:T(128)}) while((s32[]{:T(128)}, bf16[512,512]{1,0:T(8,128)(2,1)}, s32[4,2]{0,1:T(2,128)S(1)}, bf16[4,256,256]{2,1,0:T(8,128)(2,1)S(1)}, s32[]{:T(128)}) %tuple.108), condition=%wide.while_cond.2, body=%wide.while_body.2.sunk | while | flops 2 | bytes 262261 | solution.py:158
  120.8 2.3 %bitcast_dynamic-update-slice_fusion.10 = bf16[4,256,256]{2,1,0:T(8,128)(2,1)S(1)} fusion(bf16[4,256,256]{2,1,0:T(8,128)(2,1)S(1)} %get-tuple-element.279, s32[]{:T(128)S(6)} %copy.165, bf16[512,512]{1,0:T(8,128)(2,1)} %get-tuple-element.282, s32[]{:T(128)} %bitcast.96, s32[]{:T(128)} %bitcast.97), kind=kLoop, calls=%fused_computation.4.clone.1 | loop fusion | bytes 262156 | tf_op jit(solution)/shard_map/vmap()/gather
  123.8 2.3 %bitcast_dynamic-update-slice_fusion.10 = bf16[4,256,256]{2,1,0:T(8,128)(2,1)S(1)} fusion(bf16[4,256,256]{2,1,0:T(8,128)(2,1)S(1)} %get-tuple-element.279, s32[]{:T(128)S(6)} %copy.165, bf16[512,512]{1,0:T(8,128)(2,1)} %get-tuple-element.282, s32[]{:T(128)} %bitcast.96, s32[]{:T(128)} %bitcast.97), kind=kLoop, calls=%fused_computation.4.clone.1 | loop fusion | bytes 262156 | tf_op jit(solution)/shard_map/vmap()/gather
  126.7 2.3 %bitcast_dynamic-update-slice_fusion.10 = bf16[4,256,256]{2,1,0:T(8,128)(2,1)S(1)} fusion(bf16[4,256,256]{2,1,0:T(8,128)(2,1)S(1)} %get-tuple-element.279, s32[]{:T(128)S(6)} %copy.165, bf16[512,512]{1,0:T(8,128)(2,1)} %get-tuple-element.282, s32[]{:T(128)} %bitcast.96, s32[]{:T(128)} %bitcast.97), kind=kLoop, calls=%fused_computation.4.clone.1 | loop fusion | bytes 262156 | tf_op jit(solution)/shard_map/vmap()/gather
  129.7 2.3 %bitcast_dynamic-update-slice_fusion.10 = bf16[4,256,256]{2,1,0:T(8,128)(2,1)S(1)} fusion(bf16[4,256,256]{2,1,0:T(8,128)(2,1)S(1)} %get-tuple-element.279, s32[]{:T(128)S(6)} %copy.165, bf16[512,512]{1,0:T(8,128)(2,1)} %get-tuple-element.282, s32[]{:T(128)} %bitcast.96, s32[]{:T(128)} %bitcast.97), kind=kLoop, calls=%fused_computation.4.clone.1 | loop fusion | bytes 262156 | tf_op jit(solution)/shard_map/vmap()/gather
  132.0 7.8 %while.5 = (s32[]{:T(128)}, bf16[512,512]{1,0:T(8,128)(2,1)S(1)}, s32[4,2]{0,1:T(2,128)S(1)}, bf16[4,256,256]{2,1,0:T(8,128)(2,1)S(1)}, s32[]{:T(128)}) while((s32[]{:T(128)}, bf16[512,512]{1,0:T(8,128)(2,1)S(1)}, s32[4,2]{0,1:T(2,128)S(1)}, bf16[4,256,256]{2,1,0:T(8,128)(2,1)S(1)}, s32[]{:T(128)}) %tuple.109), condition=%wide.while_cond.1, body=%wide.while_body.1.sunk | while | flops 2 | bytes 262261 | solution.py:158
  138.5 1.3 bitcast_dynamic-update-slice_fusion.9
  139.9 7.8 %while.4 = (s32[]{:T(128)}, bf16[512,512]{1,0:T(8,128)(2,1)S(1)}, s32[4,2]{0,1:T(2,128)S(1)}, bf16[4,256,256]{2,1,0:T(8,128)(2,1)S(1)}, s32[]{:T(128)}) while((s32[]{:T(128)}, bf16[512,512]{1,0:T(8,128)(2,1)S(1)}, s32[4,2]{0,1:T(2,128)S(1)}, bf16[4,256,256]{2,1,0:T(8,128)(2,1)S(1)}, s32[]{:T(128)}) %tuple.110), condition=%wide.while_cond, body=%wide.while_body.sunk | while | flops 2 | bytes 262261 | solution.py:158
  149.1 4.8 %add_convert_fusion.3 = (bf16[4,256,256]{1,2,0:T(8,128)(2,1)S(1)}, bf16[4,256,256]{1,2,0:T(8,128)(2,1)S(1)}) fusion(f32[256,256]{0,1:T(8,128)S(1)} %copy.105, s32[4,256]{1,0:T(4,128)S(1)} %get-tuple-element.134, s32[4,256]{1,0:T(4,128)S(1)} %get-tuple-element.135, f32[256,256]{0,1:T(8,128)S(1)} %copy.104), kind=kLoop, calls=%fused_computation.206 | loop fusion | flops 5767168 | bytes 1581056 | tf_op jit(solution)/shard_map/convert_element_type | solution.py:76
  155.7 4.1 %fusion.30 = (bf16[4,256,256]{2,1,0:T(8,128)(2,1)S(1)}, bf16[4,256,256]{2,1,0:T(8,128)(2,1)S(1)}) fusion(bf16[4,256,256]{2,1,0:T(8,128)(2,1)S(1)} %get-tuple-element.12, f32[8,256,512]{2,1,0:T(8,128)S(1)} %fusion.77), kind=kLoop, calls=%fused_computation.63 | loop fusion | flops 2883584 | bytes 5767168 | tf_op jit(solution)/shard_map/convert_element_type | solution.py:49
  161.8 4.7 %fusion.147 = (f32[256,256]{0,1:T(8,128)S(1)}, f32[256,256]{0,1:T(8,128)S(1)}, f32[256,256]{0,1:T(8,128)S(1)}, f32[256,256]{0,1:T(8,128)S(1)}, f32[256,256]{0,1:T(8,128)S(1)}, /*index=5*/f32[256,256]{0,1:T(8,128)S(1)}) fusion(f32[]{:T(128)} %bitcast.11, s32[256]{0:T(256)S(1)} %fusion.169, f32[]{:T(128)} %bitcast.17, f32[]{:T(128)} %bitcast.14), kind=kLoop, calls=%fused_computation.227 | loop fusion | flops 983040 | bytes 1573900 | tf_op jit(solution)/shard_map/mul | solution.py:89
  168.8 4.3 %fusion.26 = (bf16[4,256,256]{2,1,0:T(8,128)(2,1)S(1)}, bf16[4,256,256]{2,1,0:T(8,128)(2,1)S(1)}) fusion(bf16[4,256,256]{2,1,0:T(8,128)(2,1)S(1)} %get-tuple-element.20, f32[8,256,512]{2,1,0:T(8,128)S(1)} %fusion.91), kind=kLoop, calls=%fused_computation.59 | loop fusion | flops 2883584 | bytes 5767168 | tf_op jit(solution)/shard_map/convert_element_type | solution.py:49
  177.4 4.1 %fusion.22 = (bf16[4,256,256]{2,1,0:T(8,128)(2,1)S(1)}, bf16[4,256,256]{2,1,0:T(8,128)(2,1)S(1)}) fusion(bf16[4,256,256]{2,1,0:T(8,128)(2,1)S(1)} %get-tuple-element.28, f32[8,256,512]{2,1,0:T(8,128)S(1)} %fusion.105), kind=kLoop, calls=%fused_computation.55 | loop fusion | flops 2883584 | bytes 5767168 | tf_op jit(solution)/shard_map/convert_element_type | solution.py:49
  185.7 4.4 %fusion.18 = (bf16[4,256,256]{2,1,0:T(8,128)(2,1)S(1)}, bf16[4,256,256]{2,1,0:T(8,128)(2,1)S(1)}) fusion(bf16[4,256,256]{2,1,0:T(8,128)(2,1)S(1)} %get-tuple-element.36, f32[8,256,512]{2,1,0:T(8,128)S(1)} %fusion.119), kind=kLoop, calls=%fused_computation.51 | loop fusion | flops 2883584 | bytes 5767168 | tf_op jit(solution)/shard_map/convert_element_type | solution.py:49
  194.1 6.8 %all-to-all-start = ((bf16[4,16,4096]{2,0,1:T(4,128)(2,1)}), bf16[4,16,4096]{2,0,1:T(4,128)(2,1)S(1)}, u32[]{:S(2)}, u32[]{:S(2)}) async-start(bf16[4,16,4096]{2,0,1:T(4,128)(2,1)} %copy.135), calls=%async_computation | async-start | bytes 1048576 | tf_op jit(solution)/shard_map/all_to_all | solution.py:165
  201.0 14.1 %all-to-all-done = bf16[4,16,4096]{2,0,1:T(4,128)(2,1)S(1)} async-done(((bf16[4,16,4096]{2,0,1:T(4,128)(2,1)}), bf16[4,16,4096]{2,0,1:T(4,128)(2,1)S(1)}, u32[]{:S(2)}, u32[]{:S(2)}) %all-to-all-start) | async-done | bytes 524320 | tf_op jit(solution)/shard_map/all_to_all | solution.py:165
  215.9 1.5 pad_maximum_fusion
  (102 shorter events, 46.7 us)
Async XLA Ops:
  9.5 98.3 %copy-start.1 = (s32[4,2]{0,1:T(2,128)S(1)}, s32[4,2]{0,1:T(2,128)}, u32[]{:S(2)}) copy-start(s32[4,2]{0,1:T(2,128)} %param.15) | copy-start | bytes 100
  106.6 12.8 %copy-start = (f32[3]{0:T(128)S(1)}, f32[3]{0:T(128)}, u32[]{:S(2)}) copy-start(f32[3]{0:T(128)} %param.17) | copy-start | bytes 40
  119.4 29.5 %copy-start.2 = (s32[4,2]{0,1:T(2,128)S(1)}, s32[4,2]{0,1:T(2,128)}, u32[]{:S(2)}) copy-start(s32[4,2]{0,1:T(2,128)} %param.16) | copy-start | bytes 100
  194.1 21.1 %all-to-all-start = ((bf16[4,16,4096]{2,0,1:T(4,128)(2,1)}), bf16[4,16,4096]{2,0,1:T(4,128)(2,1)S(1)}, u32[]{:S(2)}, u32[]{:S(2)}) async-start(bf16[4,16,4096]{2,0,1:T(4,128)(2,1)} %copy.135), calls=%async_computation | async-start | bytes 1048576 | tf_op jit(solution)/shard_map/all_to_all | solution.py:165
where the time goes:
time: 218 us; the launch traced here: 217 us
  blocking collectives  97.1 us (45%)
  local copies, waits for them, and re-layouts  44.5 us (20%)
  other arithmetic  36.9 us (17%)
  matrix products  17.2 us (8%)
  waiting for transfers between devices  14.1 us (6%)
  starting transfers between devices  6.8 us (3%)
    psum x1, blocking collectives, on_device(): lax.psum(partial_field, 'probe').astype(jnp.bfloat16).reshape(SLICES, G, G)  97.1 us
    gather x48, local copies, waits for them, and re-layouts  38.6 us
    convert_element_type x4, other arithmetic, transmit(): (real_part * cosine - imag_part * sine).astype(jnp.bfloat16)  17 us
    all_to_all x1, waiting for transfers between devices, on_device(): lax.all_to_all(pieces, 'probe', split_axis=1, concat_axis=0, tiled=True)  14.1 us
    all_to_all x1, starting transfers between devices, on_device(): lax.all_to_all(pieces, 'probe', split_axis=1, concat_axis=0, tiled=True)  6.8 us
    dot_general x8, matrix products, along_columns(): jnp.einsum('byx,xl->byl', stacked, matrix, preferred_element_type=jnp.flo...  6.17 us
    dot_general x8, matrix products, along_rows(): jnp.einsum('ky,byx->bkx', matrix, stacked, preferred_element_type=jnp.flo...  6.03 us
    convert_element_type x1, other arithmetic, multislice(): (probe_spectrum[0] * cosine + probe_spectrum[1] * sine).astype(jnp.bfloat16)  4.77 us
  transfers between devices with their start and end apart: 1, of which 1 were waited for; matrix products, arithmetic and copies ran while one was open for 0% of the time, Pallas kernels for 0%

commit v1 on v0

--- a/solution.py
+++ b/solution.py
@@ -162,7 +162,14 @@
     intensity = multislice(probe_spectrum, probe_shifts, windows, slice_phase)
     local_count = intensity.shape[0]
     pieces = intensity.reshape(local_count, devices, W * W // devices)
-    return scan_transform(lax.all_to_all(pieces, "probe", split_axis=1, concat_axis=0, tiled=True))
+    return scan_transform(
+        jnp.concatenate(
+            lax.all_to_all(
+                jnp.stack(jnp.split(pieces, lax.axis_size("probe"), axis=1)), "probe", 0, 0
+            ),
+            axis=0,
+        )
+    )
 
 
 def solution(mesh):

time: 218 us -> 231 us (1.060)
  local copies, waits for them, and re-layouts: 44.5 us -> 57.1 us
    unnamed x10 -> x25, local copies, waits for them, and re-layouts: 0.17 us -> 10.1 us
    gather x48, local copies, waits for them, and re-layouts: 38.6 us -> 41 us
where the time goes in v1:
time: 231 us; the launch traced here: 230 us
  blocking collectives  97.1 us (42%)
  local copies, waits for them, and re-layouts  57.1 us (25%)
  other arithmetic  36.9 us (16%)
  matrix products  17.2 us (7%)
  waiting for transfers between devices  14.1 us (6%)
  starting transfers between devices  6.8 us (3%)
    psum x1, blocking collectives, on_device(): lax.psum(partial_field, 'probe').astype(jnp.bfloat16).reshape(SLICES, G, G)  97.1 us
    gather x48, local copies, waits for them, and re-layouts  41 us
    convert_element_type x4, other arithmetic, transmit(): (real_part * cosine - imag_part * sine).astype(jnp.bfloat16)  17 us
    all_to_all x1, waiting for transfers between devices, on_device(): lax.all_to_all(jnp.stack(jnp.split(pieces, lax.axis_size('probe'), axis=1...  14.1 us
    unnamed x25, local copies, waits for them, and re-layouts  10.1 us
    all_to_all x1, starting transfers between devices, on_device(): lax.all_to_all(jnp.stack(jnp.split(pieces, lax.axis_size('probe'), axis=1...  6.8 us
    dot_general x8, matrix products, along_columns(): jnp.einsum('byx,xl->byl', stacked, matrix, preferred_element_type=jnp.flo...  6.17 us
    dot_general x8, matrix products, along_rows(): jnp.einsum('ky,byx->bkx', matrix, stacked, preferred_element_type=jnp.flo...  6.03 us
  transfers between devices with their start and end apart: 1, of which 1 were waited for; matrix products, arithmetic and copies ran while one was open for 0% of the time, Pallas kernels for 0%

profile of v1, /device:TPU:0, one launch (start us, length us, event | category | flops | bytes accessed | tf_op | source)
XLA Modules:
  0.0 230.0 jit_solution(14536529735462952546)
XLA Ops:
  5.0 4.5 %fusion.16 = f32[2048,512]{1,0:T(8,128)} fusion(bf16[2048,1024]{1,0:T(8,128)(2,1)S(1)} %bitcast.130, f32[1024]{0:T(1024)S(1)} %multiply_divide_fusion, f32[1024]{0:T(1024)S(1)} %bitcast.132), kind=kOutput, calls=%fused_computation.49 | convolution fusion | flops 2150105088 | bytes 8396800 | tf_op jit(solution)/shard_map/dot_general | solution.py:152
  9.5 97.1 %all-reduce.1 = bf16[2048,512]{1,0:T(8,128)(2,1)S(1)} all-reduce(f32[2048,512]{1,0:T(8,128)} %fusion.16), channel_id=1, replica_groups=mesh['groups'=2,'probe'=16] {'probe'}, use_global_device_ids=true, to_apply=%region_2.0 | all-reduce | flops 1048576 | bytes 6291456 | tf_op jit(solution)/shard_map/psum | solution.py:153
  107.8 12.0 %while.7 = (s32[]{:T(128)}, bf16[512,512]{1,0:T(8,128)(2,1)}, s32[4,2]{0,1:T(2,128)S(1)}, bf16[4,256,256]{2,1,0:T(8,128)(2,1)S(1)}, s32[]{:T(128)}) while((s32[]{:T(128)}, bf16[512,512]{1,0:T(8,128)(2,1)}, s32[4,2]{0,1:T(2,128)S(1)}, bf16[4,256,256]{2,1,0:T(8,128)(2,1)S(1)}, s32[]{:T(128)}) %tuple.111), condition=%wide.while_cond.3, body=%wide.while_body.3.sunk | while | flops 2 | bytes 262261 | solution.py:158
  108.5 2.3 %bitcast_dynamic-update-slice_fusion.11 = bf16[4,256,256]{2,1,0:T(8,128)(2,1)S(1)} fusion(bf16[4,256,256]{2,1,0:T(8,128)(2,1)S(1)} %get-tuple-element.280, s32[]{:T(128)S(6)} %copy.742, bf16[512,512]{1,0:T(8,128)(2,1)} %get-tuple-element.283, s32[]{:T(128)} %bitcast.128, s32[]{:T(128)} %bitcast.129), kind=kLoop, calls=%fused_computation.6.clone.1 | loop fusion | bytes 262156 | tf_op jit(solution)/shard_map/vmap()/gather
  111.5 2.3 %bitcast_dynamic-update-slice_fusion.11 = bf16[4,256,256]{2,1,0:T(8,128)(2,1)S(1)} fusion(bf16[4,256,256]{2,1,0:T(8,128)(2,1)S(1)} %get-tuple-element.280, s32[]{:T(128)S(6)} %copy.742, bf16[512,512]{1,0:T(8,128)(2,1)} %get-tuple-element.283, s32[]{:T(128)} %bitcast.128, s32[]{:T(128)} %bitcast.129), kind=kLoop, calls=%fused_computation.6.clone.1 | loop fusion | bytes 262156 | tf_op jit(solution)/shard_map/vmap()/gather
  114.5 2.3 %bitcast_dynamic-update-slice_fusion.11 = bf16[4,256,256]{2,1,0:T(8,128)(2,1)S(1)} fusion(bf16[4,256,256]{2,1,0:T(8,128)(2,1)S(1)} %get-tuple-element.280, s32[]{:T(128)S(6)} %copy.742, bf16[512,512]{1,0:T(8,128)(2,1)} %get-tuple-element.283, s32[]{:T(128)} %bitcast.128, s32[]{:T(128)} %bitcast.129), kind=kLoop, calls=%fused_computation.6.clone.1 | loop fusion | bytes 262156 | tf_op jit(solution)/shard_map/vmap()/gather
  117.5 2.3 %bitcast_dynamic-update-slice_fusion.11 = bf16[4,256,256]{2,1,0:T(8,128)(2,1)S(1)} fusion(bf16[4,256,256]{2,1,0:T(8,128)(2,1)S(1)} %get-tuple-element.280, s32[]{:T(128)S(6)} %copy.742, bf16[512,512]{1,0:T(8,128)(2,1)} %get-tuple-element.283, s32[]{:T(128)} %bitcast.128, s32[]{:T(128)} %bitcast.129), kind=kLoop, calls=%fused_computation.6.clone.1 | loop fusion | bytes 262156 | tf_op jit(solution)/shard_map/vmap()/gather
  120.5 12.4 %while.6 = (s32[]{:T(128)}, bf16[512,512]{1,0:T(8,128)(2,1)}, s32[4,2]{0,1:T(2,128)S(1)}, bf16[4,256,256]{2,1,0:T(8,128)(2,1)S(1)}, s32[]{:T(128)}) while((s32[]{:T(128)}, bf16[512,512]{1,0:T(8,128)(2,1)}, s32[4,2]{0,1:T(2,128)S(1)}, bf16[4,256,256]{2,1,0:T(8,128)(2,1)S(1)}, s32[]{:T(128)}) %tuple.123), condition=%wide.while_cond.2, body=%wide.while_body.2.sunk | while | flops 2 | bytes 262261 | solution.py:158
  121.2 2.4 %bitcast_dynamic-update-slice_fusion.10 = bf16[4,256,256]{2,1,0:T(8,128)(2,1)S(1)} fusion(bf16[4,256,256]{2,1,0:T(8,128)(2,1)S(1)} %get-tuple-element.295, s32[]{:T(128)S(6)} %copy.748, bf16[512,512]{1,0:T(8,128)(2,1)} %get-tuple-element.298, s32[]{:T(128)} %bitcast.125, s32[]{:T(128)} %bitcast.126), kind=kLoop, calls=%fused_computation.4.clone.1 | loop fusion | bytes 262156 | tf_op jit(solution)/shard_map/vmap()/gather
  124.3 2.4 %bitcast_dynamic-update-slice_fusion.10 = bf16[4,256,256]{2,1,0:T(8,128)(2,1)S(1)} fusion(bf16[4,256,256]{2,1,0:T(8,128)(2,1)S(1)} %get-tuple-element.295, s32[]{:T(128)S(6)} %copy.748, bf16[512,512]{1,0:T(8,128)(2,1)} %get-tuple-element.298, s32[]{:T(128)} %bitcast.125, s32[]{:T(128)} %bitcast.126), kind=kLoop, calls=%fused_computation.4.clone.1 | loop fusion | bytes 262156 | tf_op jit(solution)/shard_map/vmap()/gather
  127.3 2.4 %bitcast_dynamic-update-slice_fusion.10 = bf16[4,256,256]{2,1,0:T(8,128)(2,1)S(1)} fusion(bf16[4,256,256]{2,1,0:T(8,128)(2,1)S(1)} %get-tuple-element.295, s32[]{:T(128)S(6)} %copy.748, bf16[512,512]{1,0:T(8,128)(2,1)} %get-tuple-element.298, s32[]{:T(128)} %bitcast.125, s32[]{:T(128)} %bitcast.126), kind=kLoop, calls=%fused_computation.4.clone.1 | loop fusion | bytes 262156 | tf_op jit(solution)/shard_map/vmap()/gather
  130.4 2.4 %bitcast_dynamic-update-slice_fusion.10 = bf16[4,256,256]{2,1,0:T(8,128)(2,1)S(1)} fusion(bf16[4,256,256]{2,1,0:T(8,128)(2,1)S(1)} %get-tuple-element.295, s32[]{:T(128)S(6)} %copy.748, bf16[512,512]{1,0:T(8,128)(2,1)} %get-tuple-element.298, s32[]{:T(128)} %bitcast.125, s32[]{:T(128)} %bitcast.126), kind=kLoop, calls=%fused_computation.4.clone.1 | loop fusion | bytes 262156 | tf_op jit(solution)/shard_map/vmap()/gather
  132.9 8.5 %while.5 = (s32[]{:T(128)}, bf16[512,512]{1,0:T(8,128)(2,1)S(1)}, s32[4,2]{0,1:T(2,128)S(1)}, bf16[4,256,256]{2,1,0:T(8,128)(2,1)S(1)}, s32[]{:T(128)}) while((s32[]{:T(128)}, bf16[512,512]{1,0:T(8,128)(2,1)S(1)}, s32[4,2]{0,1:T(2,128)S(1)}, bf16[4,256,256]{2,1,0:T(8,128)(2,1)S(1)}, s32[]{:T(128)}) %tuple.124), condition=%wide.while_cond.1, body=%wide.while_body.1.sunk | while | flops 2 | bytes 262261 | solution.py:158
  133.6 1.4 bitcast_dynamic-update-slice_fusion.9
  141.4 8.5 %while.4 = (s32[]{:T(128)}, bf16[512,512]{1,0:T(8,128)(2,1)S(1)}, s32[4,2]{0,1:T(2,128)S(1)}, bf16[4,256,256]{2,1,0:T(8,128)(2,1)S(1)}, s32[]{:T(128)}) while((s32[]{:T(128)}, bf16[512,512]{1,0:T(8,128)(2,1)S(1)}, s32[4,2]{0,1:T(2,128)S(1)}, bf16[4,256,256]{2,1,0:T(8,128)(2,1)S(1)}, s32[]{:T(128)}) %tuple.125), condition=%wide.while_cond, body=%wide.while_body.sunk | while | flops 2 | bytes 262261 | solution.py:158
  151.4 4.8 %add_convert_fusion.3 = (bf16[4,256,256]{1,2,0:T(8,128)(2,1)S(1)}, bf16[4,256,256]{1,2,0:T(8,128)(2,1)S(1)}) fusion(f32[256,256]{0,1:T(8,128)S(1)} %copy.657, s32[4,256]{1,0:T(4,128)S(1)} %get-tuple-element.150, s32[4,256]{1,0:T(4,128)S(1)} %get-tuple-element.151, f32[256,256]{0,1:T(8,128)S(1)} %copy.656), kind=kLoop, calls=%fused_computation.206 | loop fusion | flops 5767168 | bytes 1581056 | tf_op jit(solution)/shard_map/convert_element_type | solution.py:76
  158.0 4.1 %fusion.30 = (bf16[4,256,256]{2,1,0:T(8,128)(2,1)S(1)}, bf16[4,256,256]{2,1,0:T(8,128)(2,1)S(1)}) fusion(bf16[4,256,256]{2,1,0:T(8,128)(2,1)S(1)} %get-tuple-element.12, f32[8,256,512]{2,1,0:T(8,128)S(1)} %fusion.77), kind=kLoop, calls=%fused_computation.63 | loop fusion | flops 2883584 | bytes 5767168 | tf_op jit(solution)/shard_map/convert_element_type | solution.py:49
  164.1 4.7 %fusion.147 = (f32[256,256]{0,1:T(8,128)S(1)}, f32[256,256]{0,1:T(8,128)S(1)}, f32[256,256]{0,1:T(8,128)S(1)}, f32[256,256]{0,1:T(8,128)S(1)}, f32[256,256]{0,1:T(8,128)S(1)}, /*index=5*/f32[256,256]{0,1:T(8,128)S(1)}) fusion(f32[]{:T(128)} %bitcast.11, s32[256]{0:T(256)S(1)} %fusion.169, f32[]{:T(128)} %bitcast.17, f32[]{:T(128)} %bitcast.14), kind=kLoop, calls=%fused_computation.227 | loop fusion | flops 983040 | bytes 1573900 | tf_op jit(solution)/shard_map/mul | solution.py:89
  171.1 4.3 %fusion.26 = (bf16[4,256,256]{2,1,0:T(8,128)(2,1)S(1)}, bf16[4,256,256]{2,1,0:T(8,128)(2,1)S(1)}) fusion(bf16[4,256,256]{2,1,0:T(8,128)(2,1)S(1)} %get-tuple-element.20, f32[8,256,512]{2,1,0:T(8,128)S(1)} %fusion.91), kind=kLoop, calls=%fused_computation.59 | loop fusion | flops 2883584 | bytes 5767168 | tf_op jit(solution)/shard_map/convert_element_type | solution.py:49
  179.6 4.1 %fusion.22 = (bf16[4,256,256]{2,1,0:T(8,128)(2,1)S(1)}, bf16[4,256,256]{2,1,0:T(8,128)(2,1)S(1)}) fusion(bf16[4,256,256]{2,1,0:T(8,128)(2,1)S(1)} %get-tuple-element.28, f32[8,256,512]{2,1,0:T(8,128)S(1)} %fusion.105), kind=kLoop, calls=%fused_computation.55 | loop fusion | flops 2883584 | bytes 5767168 | tf_op jit(solution)/shard_map/convert_element_type | solution.py:49
  188.0 4.4 %fusion.18 = (bf16[4,256,256]{2,1,0:T(8,128)(2,1)S(1)}, bf16[4,256,256]{2,1,0:T(8,128)(2,1)S(1)}) fusion(bf16[4,256,256]{2,1,0:T(8,128)(2,1)S(1)} %get-tuple-element.36, f32[8,256,512]{2,1,0:T(8,128)S(1)} %fusion.119), kind=kLoop, calls=%fused_computation.51 | loop fusion | flops 2883584 | bytes 5767168 | tf_op jit(solution)/shard_map/convert_element_type | solution.py:49
  206.7 6.8 %all-to-all-start = ((bf16[16,4,1,4096]{3,1,2,0:T(4,128)(2,1)}), bf16[16,4,1,4096]{3,1,2,0:T(4,128)(2,1)S(1)}, u32[]{:S(2)}, u32[]{:S(2)}) async-start(bf16[16,4,1,4096]{3,1,2,0:T(4,128)(2,1)} %constant_dynamic-update-slice_fusion), calls=%async_computation | async-start | bytes 1048576 | tf_op jit(solution)/shard_map/all_to_all | solution.py:167
  213.6 14.1 %all-to-all-done = bf16[16,4,1,4096]{3,1,2,0:T(4,128)(2,1)S(1)} async-done(((bf16[16,4,1,4096]{3,1,2,0:T(4,128)(2,1)}), bf16[16,4,1,4096]{3,1,2,0:T(4,128)(2,1)S(1)}, u32[]{:S(2)}, u32[]{:S(2)}) %all-to-all-start) | async-done | bytes 524320 | tf_op jit(solution)/shard_map/all_to_all | solution.py:167
  228.5 1.5 pad_maximum_fusion
  (118 shorter events, 58.4 us)
Async XLA Ops:
  9.5 98.2 %copy-start.1 = (s32[4,2]{0,1:T(2,128)S(1)}, s32[4,2]{0,1:T(2,128)}, u32[]{:S(2)}) copy-start(s32[4,2]{0,1:T(2,128)} %param.15) | copy-start | bytes 100
  106.6 13.2 %copy-start = (f32[3]{0:T(128)S(1)}, f32[3]{0:T(128)}, u32[]{:S(2)}) copy-start(f32[3]{0:T(128)} %param.17) | copy-start | bytes 40
  119.8 31.3 %copy-start.2 = (s32[4,2]{0,1:T(2,128)S(1)}, s32[4,2]{0,1:T(2,128)}, u32[]{:S(2)}) copy-start(s32[4,2]{0,1:T(2,128)} %param.16) | copy-start | bytes 100
  206.7 21.1 %all-to-all-start = ((bf16[16,4,1,4096]{3,1,2,0:T(4,128)(2,1)}), bf16[16,4,1,4096]{3,1,2,0:T(4,128)(2,1)S(1)}, u32[]{:S(2)}, u32[]{:S(2)}) async-start(bf16[16,4,1,4096]{3,1,2,0:T(4,128)(2,1)} %constant_dynamic-update-slice_fusion), calls=%async_computation | async-start | bytes 1048576 | tf_op jit(solution)/shard_map/all_to_all | solution.py:167
